TPU v7x, 512 devices: a whole 4x8x8 slice. The times are simulated.
512 devices in a mesh: grp: 16 (over y, x_hi), pos: 32 (over x_lo, z, core).
Axes of the slice: x: 4 (x_hi: 2, x_lo: 2; x = x_hi * 2 + x_lo), y: 8, z: 8, core: 2. Of those that a mesh axis runs over, the one named last changes fastest.
Arguments:
- features: bfloat16 [2, 2048, 512, 448], P(None, ('grp', 'pos'))
- channel_index: int32 [100], replicated, may hold values from 0 to 447, as said below
Outputs:
- factor: float32 [512, 100, 100], P('pos')
- mean_vec: float32 [512, 100], P('pos')
Inputs may be any that keep to these rules, and one draw needn't show every extreme that they name: `channel_index`: 100 distinct channel numbers; 0 and 447 are always among them.
All inputs are finite; a program needn't handle non-finite values.
Results may differ from a plain program's by a relative error of at most 0.0003.
Values may be sent and summed in bfloat16 or wider, within the bound.
A program may use at most 64 MiB of HBM per device.

v0:
```python
import jax
import jax.numpy as jnp
from jax import lax
from jax.sharding import PartitionSpec as P

RIDGE = 0.01


def moments(received):
    samples = received.reshape(received.shape[0], received.shape[2], received.shape[3])
    second_moment = jnp.einsum("ipc,ipd->pcd", samples, samples, preferred_element_type=jnp.float32)
    column_sums = jnp.sum(samples.astype(jnp.float32), axis=0)
    return (second_moment, column_sums)


def combine(second_moment, column_sums):
    return (
        lax.psum_scatter(second_moment, "grp", scatter_dimension=0, tiled=True),
        lax.psum_scatter(column_sums, "grp", scatter_dimension=0, tiled=True),
    )


def factorize(second_moment, column_sums, image_total):
    mean_vec = column_sums / image_total
    outer = image_total * mean_vec[:, :, None] * mean_vec[:, None, :]
    identity = jnp.eye(mean_vec.shape[1], dtype=jnp.float32)
    covariance = (second_moment - outer) / (image_total - 1) + RIDGE * identity
    return (jnp.linalg.cholesky(covariance), mean_vec)


def local(features, channel_index):
    pos_count = lax.axis_size("pos")
    grp_count = lax.axis_size("grp")
    batch_total, img_local, positions, width = features.shape
    keep_count = channel_index.shape[0]
    selector = (
        lax.broadcasted_iota(jnp.int32, (width, keep_count), 0) == channel_index[None, :]
    ).astype(jnp.bfloat16)
    image_total = batch_total * img_local * pos_count * grp_count
    chosen_list = []
    for batch_index in range(batch_total):
        flat = features[batch_index].reshape(img_local * positions, width)
        chosen = jnp.dot(flat, selector, preferred_element_type=jnp.float32).astype(jnp.bfloat16)
        chosen_list.append(chosen)
    partial_list = []
    for chosen in chosen_list:
        shaped = chosen.reshape(img_local, pos_count, positions // pos_count, keep_count)
        partial_list.append(
            moments(lax.all_to_all(shaped, "pos", split_axis=1, concat_axis=0, tiled=True))
        )
    shares = [combine(pair[0], pair[1]) for pair in partial_list]
    second_moment = shares[0][0]
    column_sums = shares[0][1]
    for pair in shares[1:]:
        second_moment = second_moment + pair[0]
        column_sums = column_sums + pair[1]
    factor, mean_vec = factorize(second_moment, column_sums, image_total)
    factor, mean_vec = (
        lax.all_gather(factor, "grp", axis=0, tiled=True),
        lax.all_gather(mean_vec, "grp", axis=0, tiled=True),
    )
    return (factor, mean_vec)


def solution(mesh):
    return jax.shard_map(
        local,
        mesh=mesh,
        in_specs=(P(None, ("grp", "pos"), None, None), P()),
        out_specs=(P("pos", None, None), P("pos", None)),
        check_vma=False,
    )
```

profile of v0, /device:TPU:64, one launch (start us, length us, event | category | flops | bytes accessed | tf_op | source)
XLA Modules:
  0.0 289.7 jit_solution(10344877939015737435)
XLA Ops:
  7.2 2.4 fusion.10
  9.6 1.4 copy.28
  11.0 0.0 copy-start
  11.0 0.5 copy.44
  11.5 0.1 copy-done
  11.7 0.5 fusion
  12.1 0.3 copy.29
  12.4 0.9 copy.30
  13.3 11.1 %all-to-all-start = ((bf16[4,32,16,100]{3,2,0,1:T(8,128)(2,1)}), bf16[4,32,16,100]{3,2,0,1:T(8,128)(2,1)S(1)}, u32[]{:S(2)}, u32[]{:S(2)}) async-start(bf16[4,32,16,100]{3,2,0,1:T(8,128)(2,1)} %copy.30), calls=%async_computation | async-start | bytes 1048576 | tf_op jit(solution)/shard_map/all_to_all | solution.py:49
  24.3 1.4 copy.33
  25.7 0.5 copy.45
  26.3 0.5 fusion.1
  26.7 0.3 copy.34
  27.0 0.9 copy.35
  27.9 14.2 %all-to-all-done = bf16[4,32,16,100]{3,2,0,1:T(8,128)(2,1)S(1)} async-done(((bf16[4,32,16,100]{3,2,0,1:T(8,128)(2,1)}), bf16[4,32,16,100]{3,2,0,1:T(8,128)(2,1)S(1)}, u32[]{:S(2)}, u32[]{:S(2)}) %all-to-all-start) | async-done | bytes 409632 | tf_op jit(solution)/shard_map/all_to_all | solution.py:49
  42.1 4.5 %all-to-all-start.1 = ((bf16[4,32,16,100]{3,2,0,1:T(8,128)(2,1)}), bf16[4,32,16,100]{3,2,0,1:T(8,128)(2,1)S(1)}, u32[]{:S(2)}, u32[]{:S(2)}) async-start(bf16[4,32,16,100]{3,2,0,1:T(8,128)(2,1)} %copy.35), calls=%async_computation.1 | async-start | bytes 1048576 | tf_op jit(solution)/shard_map/all_to_all | solution.py:49
  46.6 0.0 reduce-scatter.4.cloned.1.call-start
  46.6 0.4 fusion.3
  47.0 17.4 %all-to-all-done.1 = bf16[4,32,16,100]{3,2,0,1:T(8,128)(2,1)S(1)} async-done(((bf16[4,32,16,100]{3,2,0,1:T(8,128)(2,1)}), bf16[4,32,16,100]{3,2,0,1:T(8,128)(2,1)S(1)}, u32[]{:S(2)}, u32[]{:S(2)}) %all-to-all-start.1) | async-done | bytes 409632 | tf_op jit(solution)/shard_map/all_to_all | solution.py:49
  64.4 0.4 convolution_add_fusion
  64.9 1.2 copy.38
  66.1 0.0 reduce-scatter.4.cloned.1.call-update
  66.1 1.3 dynamic-slice
  67.4 0.2 convert_reduce_fusion
  67.6 0.2 convert_reduce_fusion.1
  67.7 42.8 %all-reduce.1 = f32[16,100]{1,0:T(8,128)S(1)} all-reduce(f32[16,100]{1,0:T(8,128)S(1)} %add.31), channel_id=5, replica_groups=mesh['grp'=16,'pos'=32] {'grp'}, use_global_device_ids=true, to_apply=%region_3.0.clone | all-reduce | flops 1600 | bytes 12800
  110.5 0.7 fusion.8
  111.2 35.3 %all-gather = f32[16,1,100]{2,1,0:T(1,128)S(1)} all-gather(f32[1,1,100]{2,1,0:T(1,128)S(1)} %get-tuple-element.10), channel_id=1, replica_groups=mesh['grp'=16,'pos'=32] {'grp'}, dimensions={0}, use_global_device_ids=true | all-gather | bytes 6800 | tf_op jit(solution)/shard_map/all_gather | solution.py:60
  146.5 0.7 broadcast_multiply_fusion
  147.2 78.3 %reduce-scatter.4.cloned.1.call-done = f32[1,100,100]{1,2,0:T(8,128)} async-done(((f32[16,100,100]{1,2,0:T(8,128)}), f32[1,100,100]{1,2,0:T(8,128)}) %reduce-scatter.4.cloned.1.call-update) | async-done | bytes 40016
  225.5 0.9 select_add_fusion
  226.4 0.1 copy.39
  226.5 0.9 fusion.7
  227.4 9.1 %custom-call.4 = f32[1,100,100]{2,1,0:T(8,128)S(1)} custom-call(f32[1,100,100]{2,1,0:T(8,128)S(1)} %fusion.7), custom_call_target="Cholesky" | custom-call | tf_op jit(solution)/shard_map/jit(cholesky)/cholesky | solution.py:28
  236.6 0.1 copy.40
  236.7 0.1 select_reduce_fusion
  236.8 0.6 compare_reduce_fusion
  237.4 0.7 select_select_fusion
  238.1 0.1 copy.42
  238.2 43.0 %all_gather.6 = f32[16,100,100]{2,1,0:T(8,128)S(1)} all-gather(f32[1,100,100]{2,1,0:T(8,128)S(1)} %copy.42), channel_id=1, replica_groups=mesh['grp'=16,'pos'=32] {'grp'}, dimensions={0}, use_global_device_ids=true | all-gather | bytes 680000 | tf_op jit(solution)/shard_map/all_gather | solution.py:59
  281.2 1.0 copy.43
  282.3 0.6 copy.51
  (1 shorter events, 0.0 us)
Async XLA Ops:
  11.0 0.7 copy-start
  13.3 28.8 %all-to-all-start = ((bf16[4,32,16,100]{3,2,0,1:T(8,128)(2,1)}), bf16[4,32,16,100]{3,2,0,1:T(8,128)(2,1)S(1)}, u32[]{:S(2)}, u32[]{:S(2)}) async-start(bf16[4,32,16,100]{3,2,0,1:T(8,128)(2,1)} %copy.30), calls=%async_computation | async-start | bytes 1048576 | tf_op jit(solution)/shard_map/all_to_all | solution.py:49
  42.1 22.3 %all-to-all-start.1 = ((bf16[4,32,16,100]{3,2,0,1:T(8,128)(2,1)}), bf16[4,32,16,100]{3,2,0,1:T(8,128)(2,1)S(1)}, u32[]{:S(2)}, u32[]{:S(2)}) async-start(bf16[4,32,16,100]{3,2,0,1:T(8,128)(2,1)} %copy.35), calls=%async_computation.1 | async-start | bytes 1048576 | tf_op jit(solution)/shard_map/all_to_all | solution.py:49
  46.6 178.9 %reduce-scatter.4.cloned.1.call-start = ((), (), s32[]{:S(2)}) async-start(), calls=%async_computation.3 | async-start | bytes 905216
Sparse Core Ops, SparseCore 0:
  66.3 159.2 reduce-scatter.3
where the time goes:
time: 290 us
  blocking collectives  121 us (42%)
  waiting for transfers between devices  110 us (38%)
  starting transfers between devices  15.6 us (5%)
  between operations  14.2 us (5%)
  other arithmetic  14 us (5%)
  local copies, waits for them, and re-layouts  13.2 us (5%)
    unnamed x2, waiting for transfers between devices  78.3 us
    all_gather x1, blocking collectives, local(): lax.all_gather(factor, 'grp', axis=0, tiled=True)  43 us
    unnamed x1, blocking collectives  42.8 us
    all_gather x1, blocking collectives, local(): lax.all_gather(mean_vec, 'grp', axis=0, tiled=True)  35.3 us
    all_to_all x2, waiting for transfers between devices, local(): lax.all_to_all(shaped, 'pos', split_axis=1, concat_axis=0, tiled=True)  31.6 us
    all_to_all x2, starting transfers between devices, local(): lax.all_to_all(shaped, 'pos', split_axis=1, concat_axis=0, tiled=True)  15.5 us
    another operation x3, other arithmetic, factorize(): return (jnp.linalg.cholesky(covariance), mean_vec)  9.91 us
  transfers between devices with their start and end apart: 3, of which 3 were waited for; matrix products, arithmetic and copies ran while one was open for 2% of the time, Pallas kernels for 0%

commit v1 on v0

--- a/solution.py
+++ b/solution.py
@@ -46,7 +46,14 @@
     for chosen in chosen_list:
         shaped = chosen.reshape(img_local, pos_count, positions // pos_count, keep_count)
         partial_list.append(
-            moments(lax.all_to_all(shaped, "pos", split_axis=1, concat_axis=0, tiled=True))
+            moments(
+                jnp.concatenate(
+                    lax.all_to_all(
+                        jnp.stack(jnp.split(shaped, lax.axis_size("pos"), axis=1)), "pos", 0, 0
+                    ),
+                    axis=0,
+                )
+            )
         )
     shares = [combine(pair[0], pair[1]) for pair in partial_list]
     second_moment = shares[0][0]

time: 290 us -> 317 us (1.093)
  local copies, waits for them, and re-layouts: 13.2 us -> 50.1 us
  waiting for transfers between devices: 110 us -> 95.6 us
  starting transfers between devices: 15.6 us -> 19.4 us
    unnamed x7 -> x69, local copies, waits for them, and re-layouts: 4.08 us -> 41.5 us
    all_to_all x2, waiting for transfers between devices: 31.6 us -> 17.3 us  [local(): lax.all_to_all(jnp.stack(jnp.split(shaped, lax.axis_size('pos'), axis=1))...]
    all_to_all x2, starting transfers between devices: 15.5 us -> 19.4 us  [local(): lax.all_to_all(jnp.stack(jnp.split(shaped, lax.axis_size('pos'), axis=1))...]
  transfers between devices with their start and end apart: 3 -> 3, of which waited for: 3 -> 2; matrix products, arithmetic and copies ran while one was open for 2% -> 8% of each run, Pallas kernels for 0% -> 0%
where the time goes in v1:
time: 317 us; the launch traced here: 316 us
  blocking collectives  121 us (38%)
  waiting for transfers between devices  95.6 us (30%)
  local copies, waits for them, and re-layouts  50.1 us (16%)
  starting transfers between devices  19.4 us (6%)
  between operations  14.2 us (4%)
  other arithmetic  14 us (4%)
    unnamed x2, waiting for transfers between devices  78.3 us
    all_gather x1, blocking collectives, local(): lax.all_gather(factor, 'grp', axis=0, tiled=True)  43 us
    unnamed x1, blocking collectives  42.9 us
    unnamed x69, local copies, waits for them, and re-layouts  41.5 us
    all_gather x1, blocking collectives, local(): lax.all_gather(mean_vec, 'grp', axis=0, tiled=True)  35.3 us
    all_to_all x2, starting transfers between devices, local(): lax.all_to_all(jnp.stack(jnp.split(shaped, lax.axis_size('pos'), axis=1))...  19.4 us
    all_to_all x2, waiting for transfers between devices, local(): lax.all_to_all(jnp.stack(jnp.split(shaped, lax.axis_size('pos'), axis=1))...  17.3 us
    another operation x3, other arithmetic, factorize(): return (jnp.linalg.cholesky(covariance), mean_vec)  9.91 us
  transfers between devices with their start and end apart: 3, of which 2 were waited for; matrix products, arithmetic and copies ran while one was open for 8% of the time, Pallas kernels for 0%

profile of v1, /device:TPU:64, one launch (start us, length us, event | category | flops | bytes accessed | tf_op | source)
XLA Modules:
  0.0 316.4 jit_solution(1173992517850667759)
XLA Ops:
  7.2 2.4 fusion.10
  9.6 1.4 copy.148
  12.4 0.6 constant_dynamic-update-slice_fusion.31
  13.0 0.6 constant_dynamic-update-slice_fusion.30
  13.6 0.6 constant_dynamic-update-slice_fusion.29
  14.2 0.6 constant_dynamic-update-slice_fusion.28
  14.8 0.6 constant_dynamic-update-slice_fusion.27
  15.4 0.6 constant_dynamic-update-slice_fusion.26
  16.1 0.6 constant_dynamic-update-slice_fusion.25
  16.7 0.6 constant_dynamic-update-slice_fusion.24
  17.3 0.6 constant_dynamic-update-slice_fusion.23
  17.9 0.6 constant_dynamic-update-slice_fusion.22
  18.5 0.6 constant_dynamic-update-slice_fusion.21
  19.1 0.6 constant_dynamic-update-slice_fusion.20
  19.7 0.6 constant_dynamic-update-slice_fusion.19
  20.3 0.6 constant_dynamic-update-slice_fusion.18
  20.9 0.6 constant_dynamic-update-slice_fusion.17
  21.5 0.6 constant_dynamic-update-slice_fusion.16
  22.1 0.6 constant_dynamic-update-slice_fusion.15
  22.7 0.6 constant_dynamic-update-slice_fusion.14
  23.3 0.6 constant_dynamic-update-slice_fusion.13
  24.0 0.6 constant_dynamic-update-slice_fusion.12
  24.6 0.6 constant_dynamic-update-slice_fusion.11
  25.2 0.6 constant_dynamic-update-slice_fusion.10
  25.8 0.6 constant_dynamic-update-slice_fusion.9
  27.6 0.6 constant_dynamic-update-slice_fusion.6
  28.2 0.6 constant_dynamic-update-slice_fusion.5
  30.0 0.6 constant_dynamic-update-slice_fusion.2
  30.6 0.6 constant_dynamic-update-slice_fusion.1
  31.9 11.1 %all-to-all-start = ((bf16[32,4,1,16,100]{4,3,1,2,0:T(8,128)(2,1)}), bf16[32,4,1,16,100]{4,3,1,2,0:T(8,128)(2,1)S(1)}, u32[]{:S(2)}, u32[]{:S(2)}) async-start(bf16[32,4,1,16,100]{4,3,1,2,0:T(8,128)(2,1)} %constant_dynamic-update-slice_fusion), calls=%async_computation | async-start | bytes 1048576 | tf_op jit(solution)/shard_map/all_to_all | solution.py:51
  42.9 1.4 copy.182
  52.2 0.6 constant_dynamic-update-slice_fusion.52
  64.9 8.3 %all-to-all-start.1 = ((bf16[32,4,1,16,100]{4,3,1,2,0:T(8,128)(2,1)}), bf16[32,4,1,16,100]{4,3,1,2,0:T(8,128)(2,1)S(1)}, u32[]{:S(2)}, u32[]{:S(2)}) async-start(bf16[32,4,1,16,100]{4,3,1,2,0:T(8,128)(2,1)} %constant_dynamic-update-slice_fusion.32), calls=%async_computation.1 | async-start | bytes 1048576 | tf_op jit(solution)/shard_map/all_to_all | solution.py:51
  73.7 17.3 %all-to-all-done.1 = bf16[32,4,1,16,100]{4,3,1,2,0:T(8,128)(2,1)S(1)} async-done(((bf16[32,4,1,16,100]{4,3,1,2,0:T(8,128)(2,1)}), bf16[32,4,1,16,100]{4,3,1,2,0:T(8,128)(2,1)S(1)}, u32[]{:S(2)}, u32[]{:S(2)}) %all-to-all-start.1) | async-done | bytes 409632 | tf_op jit(solution)/shard_map/all_to_all | solution.py:51
  91.4 1.2 copy.216
  92.7 1.3 dynamic-slice
  94.3 42.9 %all-reduce.1 = f32[16,100]{1,0:T(8,128)S(1)} all-reduce(f32[16,100]{1,0:T(8,128)S(1)} %add.31), channel_id=5, replica_groups=mesh['grp'=16,'pos'=32] {'grp'}, use_global_device_ids=true, to_apply=%region_3.0.clone | all-reduce | flops 1600 | bytes 12800
  137.2 0.7 fusion.8
  137.8 35.3 %all-gather = f32[16,1,100]{2,1,0:T(1,128)S(1)} all-gather(f32[1,1,100]{2,1,0:T(1,128)S(1)} %get-tuple-element.10), channel_id=1, replica_groups=mesh['grp'=16,'pos'=32] {'grp'}, dimensions={0}, use_global_device_ids=true | all-gather | bytes 6800 | tf_op jit(solution)/shard_map/all_gather | solution.py:67
  173.2 0.7 broadcast_multiply_fusion
  173.8 78.3 %reduce-scatter.4.cloned.1.call-done = f32[1,100,100]{1,2,0:T(8,128)} async-done(((f32[16,100,100]{1,2,0:T(8,128)}), f32[1,100,100]{1,2,0:T(8,128)}) %reduce-scatter.4.cloned.1.call-update) | async-done | bytes 40016
  252.2 0.9 select_add_fusion
  253.2 0.9 fusion.7
  254.1 9.1 %custom-call.4 = f32[1,100,100]{2,1,0:T(8,128)S(1)} custom-call(f32[1,100,100]{2,1,0:T(8,128)S(1)} %fusion.7), custom_call_target="Cholesky" | custom-call | tf_op jit(solution)/shard_map/jit(cholesky)/cholesky | solution.py:28
  263.4 0.6 compare_reduce_fusion
  264.1 0.7 select_select_fusion
  264.9 43.0 %all_gather.6 = f32[16,100,100]{2,1,0:T(8,128)S(1)} all-gather(f32[1,100,100]{2,1,0:T(8,128)S(1)} %copy.220), channel_id=1, replica_groups=mesh['grp'=16,'pos'=32] {'grp'}, dimensions={0}, use_global_device_ids=true | all-gather | bytes 680000 | tf_op jit(solution)/shard_map/all_gather | solution.py:66
  307.9 1.0 copy.221
  (57 shorter events, 26.6 us)
Async XLA Ops:
  11.0 0.7 copy-start
  31.9 33.0 %all-to-all-start = ((bf16[32,4,1,16,100]{4,3,1,2,0:T(8,128)(2,1)}), bf16[32,4,1,16,100]{4,3,1,2,0:T(8,128)(2,1)S(1)}, u32[]{:S(2)}, u32[]{:S(2)}) async-start(bf16[32,4,1,16,100]{4,3,1,2,0:T(8,128)(2,1)} %constant_dynamic-update-slice_fusion), calls=%async_computation | async-start | bytes 1048576 | tf_op jit(solution)/shard_map/all_to_all | solution.py:51
  64.9 26.1 %all-to-all-start.1 = ((bf16[32,4,1,16,100]{4,3,1,2,0:T(8,128)(2,1)}), bf16[32,4,1,16,100]{4,3,1,2,0:T(8,128)(2,1)S(1)}, u32[]{:S(2)}, u32[]{:S(2)}) async-start(bf16[32,4,1,16,100]{4,3,1,2,0:T(8,128)(2,1)} %constant_dynamic-update-slice_fusion.32), calls=%async_computation.1 | async-start | bytes 1048576 | tf_op jit(solution)/shard_map/all_to_all | solution.py:51
  73.2 178.9 %reduce-scatter.4.cloned.1.call-start = ((), (), s32[]{:S(2)}) async-start(), calls=%async_computation.3 | async-start | bytes 905216
Sparse Core Ops, SparseCore 0:
  92.8 159.3 reduce-scatter.3
